TPU v7x, 256 devices: a whole 4x4x8 slice. The times are simulated.
256 devices in a mesh: section: 16 (over z_hi, x, core), blk: 16 (over y, z_lo).
Axes of the slice: x: 4, y: 4, z: 8 (z_hi: 2, z_lo: 4; z = z_hi * 4 + z_lo), core: 2. Of those that a mesh axis runs over, the one named last changes fastest.
Arguments:
- queries: bfloat16 [16, 2048, 4096], P('section', 'blk'), may hold values from -6 to 6
- key_heads: bfloat16 [16, 2048, 512], P('section', 'blk'), may hold values from -6 to 6
- value_per_head: bfloat16 [16, 2048, 512], P('section', 'blk'), may hold values from -6 to 6
- out_grads: bfloat16 [16, 2048, 4096], P('section', 'blk'), may hold values from -6 to 6
- segment_ids: int32 [16, 2048], P('section', 'blk'), may hold values from 0 to 127, never falling along the last dimension, each value on 1 to 64 neighbouring positions
- block_lists: int32 [16, 16, 4], P('section', 'blk'), may hold values from 0 to 15, as said below
- list_counts: int32 [16, 16], P('section', 'blk'), may hold values from 1 to 4, as said below
Outputs:
- grad_queries: bfloat16 [16, 2048, 4096], P('section', 'blk')
- grad_keys: bfloat16 [16, 2048, 512], P('section', 'blk')
- grad_values: bfloat16 [16, 2048, 512], P('section', 'blk')
Inputs may be any that keep to these rules, and one draw needn't show every extreme that they name: `block_lists`: entry 0 of row b is b itself; for b >= 1 entry 1 is block 0; entries 2 to list_counts - 1 are distinct blocks between 1 and b - 1; entries from list_counts on repeat b. `list_counts`: at least 2 for every query block after the first; the last query block of every micro-batch uses all 4 slots.
All inputs are finite; a program needn't handle non-finite values.
Results may differ from a plain program's by a relative error of at most 0.0051.
Values may be sent and summed in bfloat16 or wider, within the bound.
A program may use at most 64 MiB of HBM per device.

v0:
```python
import math
import jax
import jax.numpy as jnp
from jax import lax
from jax.sharding import PartitionSpec as P

QUERY_HEADS = 32
KEY_VALUE_HEADS = 4
HEAD_SIZE = 128
MASK_BLOCK_SIZE = 128
LIST = 4
NEG_FILL = -1e30


def from_behind(value, axis, by):
    devices = lax.axis_size(axis)
    return lax.ppermute(value, axis, [(i, (i + by) % devices) for i in range(devices)])


def allowed_mask(block_ids, listed_count, query_block, query_segs):
    slot_ok = jnp.arange(LIST, dtype=jnp.int32) < listed_count
    own_block = block_ids == query_block
    positions = jnp.arange(MASK_BLOCK_SIZE, dtype=jnp.int32)
    causal = (positions[None, :] <= positions[:, None]) & (
        query_segs[None, :] == query_segs[:, None]
    )
    earlier = block_ids < query_block
    return slot_ok[None, :, None] & jnp.where(
        own_block[None, :, None], causal[:, None, :], earlier[None, :, None]
    )


def group_terms(query_row_slice, gradient_row_slice, key_rows, value_rows, allowed):
    scale_factor = 1.0 / math.sqrt(HEAD_SIZE)
    scores = (
        jnp.einsum("ihd,ljd->hilj", query_row_slice, key_rows, preferred_element_type=jnp.float32)
        * scale_factor
    )
    scores = jnp.where(allowed[None], scores, NEG_FILL)
    largest = jnp.max(scores, axis=(2, 3), keepdims=True)
    weights = jnp.where(allowed[None], jnp.exp(scores - largest), 0.0)
    probs_full = weights / jnp.sum(weights, axis=(2, 3), keepdims=True)
    dprobs = jnp.einsum(
        "ihd,ljd->hilj", gradient_row_slice, value_rows, preferred_element_type=jnp.float32
    )
    row_delta = jnp.sum(probs_full * dprobs, axis=(2, 3), keepdims=True)
    dscores = (probs_full * (dprobs - row_delta)).astype(jnp.bfloat16)
    probs_half = probs_full.astype(jnp.bfloat16)
    query_grad = (
        jnp.einsum("hilj,ljd->ihd", dscores, key_rows, preferred_element_type=jnp.float32)
        * scale_factor
    )
    key_grad = (
        jnp.einsum("hilj,ihd->ljd", dscores, query_row_slice, preferred_element_type=jnp.float32)
        * scale_factor
    )
    value_grad = jnp.einsum(
        "hilj,ihd->ljd", probs_half, gradient_row_slice, preferred_element_type=jnp.float32
    )
    return (query_grad, key_grad, value_grad)


def per_device(
    queries, key_heads, value_per_head, out_grads, segment_ids, block_lists, list_counts
):
    local_blocks = block_lists.shape[1]
    blk_count = lax.axis_size("blk")
    blocks_all = blk_count * local_blocks
    first_local = lax.axis_index("blk") * local_blocks
    heads_per_group = QUERY_HEADS // KEY_VALUE_HEADS
    key_value_width = KEY_VALUE_HEADS * HEAD_SIZE
    ids_all = block_lists[0]
    flat_ids = ids_all.reshape(-1)
    whole_keys, whole_values = (
        lax.all_gather(key_heads, "blk", axis=1, tiled=True),
        lax.all_gather(value_per_head, "blk", axis=1, tiled=True),
    )
    listed_k = whole_keys[0].reshape(blocks_all, MASK_BLOCK_SIZE, key_value_width)[flat_ids]
    listed_v = whole_values[0].reshape(blocks_all, MASK_BLOCK_SIZE, key_value_width)[flat_ids]
    query_all = queries[0]
    grads_all = out_grads[0]
    segs_all = segment_ids[0]
    counts_all = list_counts[0]
    query_block = first_local + 0
    row_hi = MASK_BLOCK_SIZE
    allowed = allowed_mask(ids_all[0], counts_all[0], query_block, segs_all)
    query_parts = []
    key_parts = []
    value_parts = []
    for shared_key_head in range(KEY_VALUE_HEADS):
        col_lo = shared_key_head * heads_per_group * HEAD_SIZE
        col_hi = col_lo + heads_per_group * HEAD_SIZE
        query_row_slice = query_all[0:row_hi, col_lo:col_hi].reshape(
            MASK_BLOCK_SIZE, heads_per_group, HEAD_SIZE
        )
        gradient_row_slice = grads_all[0:row_hi, col_lo:col_hi].reshape(
            MASK_BLOCK_SIZE, heads_per_group, HEAD_SIZE
        )
        head_keys = listed_k[:, :, shared_key_head * HEAD_SIZE : (shared_key_head + 1) * HEAD_SIZE]
        head_values = listed_v[
            :, :, shared_key_head * HEAD_SIZE : (shared_key_head + 1) * HEAD_SIZE
        ]
        query_grad, key_grad, value_grad = group_terms(
            query_row_slice, gradient_row_slice, head_keys, head_values, allowed
        )
        query_parts.append(query_grad.reshape(MASK_BLOCK_SIZE, heads_per_group * HEAD_SIZE))
        key_parts.append(key_grad)
        value_parts.append(value_grad)
    query_parts_all = jnp.concatenate(query_parts, axis=1).astype(jnp.bfloat16)
    grad_tiles = jnp.concatenate(key_parts + value_parts, axis=2)
    query_gradient_rows = query_parts_all[None]
    placement = (jnp.arange(blocks_all, dtype=jnp.int32)[:, None] == flat_ids[None, :]).astype(
        jnp.float32
    )
    term_all = jnp.einsum("cn,nrw->crw", placement, grad_tiles, precision=lax.Precision.HIGHEST)
    summed = lax.psum_scatter(
        term_all.reshape(blocks_all * MASK_BLOCK_SIZE, 2 * key_value_width),
        "blk",
        scatter_dimension=0,
        tiled=True,
    )
    summed_half = summed.astype(jnp.bfloat16)
    key_grads = summed_half[:, :key_value_width][None]
    value_grads = summed_half[:, key_value_width:][None]
    grad_queries, grad_keys, grad_values = from_behind(
        (query_gradient_rows, key_grads, value_grads), "section", -1
    )
    return (grad_queries, grad_keys, grad_values)


def solution(mesh):
    in_specs = (
        P("section", "blk", None),
        P("section", "blk", None),
        P("section", "blk", None),
        P("section", "blk", None),
        P("section", "blk"),
        P("section", "blk", None),
        P("section", "blk"),
    )
    out_specs = (P("section", "blk", None), P("section", "blk", None), P("section", "blk", None))
    return jax.shard_map(
        per_device, mesh=mesh, in_specs=in_specs, out_specs=out_specs, check_vma=False
    )
```

profile of v0, /device:TPU:1, one launch (start us, length us, event | category | flops | bytes accessed | tf_op | source)
XLA Modules:
  0.0 443.1 jit_solution(12771451435008800897)
XLA Ops:
  9.4 1.6 copy.22
  12.2 79.5 %all-gather.3.cloned.1.call-done = bf16[1,2048,512]{2,1,0:T(8,128)(2,1)} async-done(((bf16[1,128,512]{2,1,0:T(8,128)(2,1)}), bf16[1,2048,512]{2,1,0:T(8,128)(2,1)}) %all-gather.3.cloned.1.call-update) | async-done | bytes 2097168 | tf_op jit(solution)/shard_map/all_gather | solution.py:75
  91.7 2.2 gather_fusion
  93.8 86.1 %all-gather.5.cloned.1.call-done = bf16[1,2048,512]{2,1,0:T(8,128)(2,1)} async-done(((bf16[1,128,512]{2,1,0:T(8,128)(2,1)}), bf16[1,2048,512]{2,1,0:T(8,128)(2,1)}) %all-gather.5.cloned.1.call-update) | async-done | bytes 2097168 | tf_op jit(solution)/shard_map/all_gather | solution.py:76
  179.9 2.2 gather_fusion.1
  185.5 1.7 fusion.9
  188.4 1.8 fusion.6
  191.6 1.4 fusion.3
  193.0 2.4 fusion.11
  196.8 0.7 fusion.5
  200.0 4.0 fusion.54
  204.1 8.3 %copy.44 = f32[16,128,1024]{2,1,0:T(8,128)} copy(f32[16,128,1024]{2,0,1:T(8,128)S(1)} %fusion.54) | data formatting | bytes 16777216 | tf_op jit(solution)/shard_map/cn,nrw->crw/dot_general | solution.py:115
  212.4 1.2 fusion.31
  213.6 0.9 copy.40
  214.5 1.2 fusion.28
  215.8 0.9 copy.43
  216.6 1.3 fusion.29
  218.1 1.2 fusion.30
  219.6 10.1 %collective-permute-start = (bf16[1,128,4096]{2,1,0:T(8,128)(2,1)S(1)}, bf16[1,128,4096]{2,1,0:T(8,128)(2,1)S(1)}, u32[]{:S(2)}, u32[]{:S(2)}) collective-permute-start(bf16[1,128,4096]{2,1,0:T(8,128)(2,1)S(1)} %pad_maximum_fusion), channel_id=1, source_target_pairs={{0,240},{16,0},{32,16},{48,32},{64,48},{80,64},{96,80},{112,96},{1... | collective-permute-start | bytes 3145736 | tf_op jit(solution)/shard_map/ppermute | solution.py:17
  229.6 197.7 %reduce-scatter.2.cloned.1.call-done = f32[128,1024]{1,0:T(8,128)} async-done(((f32[2048,1024]{1,0:T(8,128)}), f32[128,1024]{1,0:T(8,128)}) %reduce-scatter.2.cloned.1.call-update) | async-done | bytes 524304 | tf_op jit(solution)/shard_map/reduce_scatter | solution.py:116
  427.3 1.1 convert_element_type.44
  429.0 3.9 collective-permute-done.2
  432.9 1.4 collective-permute-done.1
  434.3 1.0 copy.116
  (75 shorter events, 14.5 us)
Async XLA Ops:
  7.2 3.8 copy-start.9
  7.2 84.5 %all-gather.3.cloned.1.call-start = ((), (), s32[]{:S(2)}) async-start(), calls=%async_computation.1 | async-start | bytes 2228224 | tf_op jit(solution)/shard_map/all_gather | solution.py:75
  7.9 172.0 %all-gather.5.cloned.1.call-start = ((), (), s32[]{:S(2)}) async-start(), calls=%async_computation.2 | async-start | bytes 2228224 | tf_op jit(solution)/shard_map/all_gather | solution.py:76
  8.7 418.6 %reduce-scatter.2.cloned.1.call-start = ((), (), s32[]{:S(2)}) async-start(), calls=%async_computation.3 | async-start | bytes 8912896 | tf_op jit(solution)/shard_map/reduce_scatter | solution.py:116
  9.4 2.3 copy-start.13
  9.4 2.4 copy-start.12
  12.0 170.5 %copy-start.5 = (bf16[128,1024]{0,1:T(8,128)(2,1)}, bf16[128,1024]{0,1:T(8,128)(2,1)S(1)}, u32[]{:S(2)}) copy-start(bf16[128,1024]{0,1:T(8,128)(2,1)S(1)} %get-tuple-element.12) | copy-start | bytes 786436
  12.1 170.9 %copy-start.3 = (bf16[128,1024]{0,1:T(8,128)(2,1)}, bf16[128,1024]{0,1:T(8,128)(2,1)S(1)}, u32[]{:S(2)}) copy-start(bf16[128,1024]{0,1:T(8,128)(2,1)S(1)} %get-tuple-element.14) | copy-start | bytes 786436
  12.1 171.7 %copy-start.7 = (bf16[128,1024]{0,1:T(8,128)(2,1)}, bf16[128,1024]{0,1:T(8,128)(2,1)S(1)}, u32[]{:S(2)}) copy-start(bf16[128,1024]{0,1:T(8,128)(2,1)S(1)} %get-tuple-element.15) | copy-start | bytes 786436
  93.8 90.0 %copy-start.2 = (bf16[4,128,512]{2,1,0:T(8,128)(2,1)}, bf16[4,128,512]{2,1,0:T(8,128)(2,1)S(1)}, u32[]{:S(2)}) copy-start(bf16[4,128,512]{2,1,0:T(8,128)(2,1)S(1)} %gather_fusion) | copy-start | bytes 1572868
  193.0 2.5 copy-start.8
  193.0 2.9 copy-start.6
  195.4 1.0 copy-start.4
  197.6 1.7 copy-start
  213.6 3.0 copy-start.1
  216.6 2.9 copy-start.10
  217.9 1.6 copy-start.11
  219.6 209.4 %collective-permute-start = (bf16[1,128,4096]{2,1,0:T(8,128)(2,1)S(1)}, bf16[1,128,4096]{2,1,0:T(8,128)(2,1)S(1)}, u32[]{:S(2)}, u32[]{:S(2)}) collective-permute-start(bf16[1,128,4096]{2,1,0:T(8,128)(2,1)S(1)} %pad_maximum_fusion), channel_id=1, source_target_pairs={{0,240},{16,0},{32,16},{48,32},{64,48},{80,64},{96,80},{112,96},{1... | collective-permute-start | bytes 3145736 | tf_op jit(solution)/shard_map/ppermute | solution.py:17
  428.4 4.5 %collective-permute-start.2 = (bf16[1,128,512]{2,1,0:T(8,128)(2,1)S(1)}, bf16[1,128,512]{2,1,0:T(8,128)(2,1)S(1)}, u32[]{:S(2)}, u32[]{:S(2)}) collective-permute-start(bf16[1,128,512]{2,1,0:T(8,128)(2,1)S(1)} %get-tuple-element.20), channel_id=1, source_target_pairs={{0,240},{16,0},{32,16},{48,32},{64,48},{80,64},{96,80},{112,96},{1... | collective-permute-start | bytes 393224 | tf_op jit(solution)/shard_map/ppermute | solution.py:17
  428.9 5.4 %collective-permute-start.1 = (bf16[1,128,512]{2,1,0:T(8,128)(2,1)S(1)}, bf16[1,128,512]{2,1,0:T(8,128)(2,1)S(1)}, u32[]{:S(2)}, u32[]{:S(2)}) collective-permute-start(bf16[1,128,512]{2,1,0:T(8,128)(2,1)S(1)} %get-tuple-element.21), channel_id=1, source_target_pairs={{0,240},{16,0},{32,16},{48,32},{64,48},{80,64},{96,80},{112,96},{1... | collective-permute-start | bytes 393224 | tf_op jit(solution)/shard_map/ppermute | solution.py:17
Sparse Core Ops, SparseCore 0:
  9.8 81.8 all-gather.2
  93.4 86.4 all-gather.4
  212.5 214.7 reduce-scatter.1
where the time goes:
time: 443 us
  waiting for transfers between devices  370 us (84%)
  matrix products  20.5 us (5%)
  local copies, waits for them, and re-layouts  20.4 us (5%)
  between operations  14.9 us (3%)
  starting transfers between devices  10.8 us (2%)
  other arithmetic  6.55 us (1%)
    reduce_scatter x1, waiting for transfers between devices, per_device(): lax.psum_scatter(term_all.reshape(blocks_all * MASK_BLOCK_SIZE, 2 * key_v...  198 us
    all_gather x1, waiting for transfers between devices, per_device(): lax.all_gather(value_per_head, 'blk', axis=1, tiled=True)  86.1 us
    all_gather x1, waiting for transfers between devices, per_device(): lax.all_gather(key_heads, 'blk', axis=1, tiled=True)  79.5 us
    ppermute x3, starting transfers between devices, from_behind(): lax.ppermute(value, axis, [(i, (i + by) % devices) for i in range(devices)])  10.6 us
  transfers between devices with their start and end apart: 6, of which 5 were waited for; matrix products, arithmetic and copies ran while one was open for 3% of the time, Pallas kernels for 0%

commit v1 on v0

--- a/solution.py
+++ b/solution.py
@@ -10,6 +10,13 @@
 MASK_BLOCK_SIZE = 128
 LIST = 4
 NEG_FILL = -1e30
+
+
+def swapped_in(value, axis, dim):
+    devices = lax.axis_size(axis)
+    blocks = jnp.stack([value for _ in range(devices)])
+    blocks = lax.all_to_all(blocks, axis, split_axis=0, concat_axis=0)
+    return jnp.concatenate(blocks, axis=dim)
 
 
 def from_behind(value, axis, by):
@@ -73,7 +80,7 @@
     flat_ids = ids_all.reshape(-1)
     whole_keys, whole_values = (
         lax.all_gather(key_heads, "blk", axis=1, tiled=True),
-        lax.all_gather(value_per_head, "blk", axis=1, tiled=True),
+        swapped_in(value_per_head, "blk", 1),
     )
     listed_k = whole_keys[0].reshape(blocks_all, MASK_BLOCK_SIZE, key_value_width)[flat_ids]
     listed_v = whole_values[0].reshape(blocks_all, MASK_BLOCK_SIZE, key_value_width)[flat_ids]

time: 443 us -> 384 us (0.87)
  waiting for transfers between devices: 370 us -> 291 us
  local copies, waits for them, and re-layouts: 20.4 us -> 27.5 us
  starting transfers between devices: 10.8 us -> 16.8 us
    all_gather x1 -> x0, waiting for transfers between devices: 86.1 us -> none  [per_device(): lax.all_gather(value_per_head, 'blk', axis=1, tiled=True)]
    all_to_all x0 -> x1, starting transfers between devices: none -> 9.37 us  [swapped_in(): blocks = lax.all_to_all(blocks, axis, split_axis=0, concat_axis=0)]
    all_gather x1, waiting for transfers between devices: 79.5 us -> 88.5 us  [per_device(): lax.all_gather(key_heads, 'blk', axis=1, tiled=True)]
  transfers between devices with their start and end apart: 6 -> 6, of which waited for: 5 -> 4; matrix products, arithmetic and copies ran while one was open for 3% -> 5% of each run, Pallas kernels for 0% -> 0%
where the time goes in v1:
time: 384 us; the launch traced here: 382 us
  waiting for transfers between devices  291 us (76%)
  local copies, waits for them, and re-layouts  27.5 us (7%)
  matrix products  24.1 us (6%)
  starting transfers between devices  16.8 us (4%)
  between operations  15.4 us (4%)
  other arithmetic  6.54 us (2%)
    reduce_scatter x1, waiting for transfers between devices, per_device(): lax.psum_scatter(term_all.reshape(blocks_all * MASK_BLOCK_SIZE, 2 * key_v...  197 us
    all_gather x1, waiting for transfers between devices, per_device(): lax.all_gather(key_heads, 'blk', axis=1, tiled=True)  88.5 us
    all_to_all x1, starting transfers between devices, swapped_in(): blocks = lax.all_to_all(blocks, axis, split_axis=0, concat_axis=0)  9.37 us
    dot_general x1, local copies, waits for them, and re-layouts, per_device(): jnp.einsum('cn,nrw->crw', placement, grad_tiles, precision=lax.Precision....  8.3 us
    unnamed x58, local copies, waits for them, and re-layouts  8.1 us
  transfers between devices with their start and end apart: 6, of which 4 were waited for; matrix products, arithmetic and copies ran while one was open for 5% of the time, Pallas kernels for 0%

profile of v1, /device:TPU:1, one launch (start us, length us, event | category | flops | bytes accessed | tf_op | source)
XLA Modules:
  0.0 381.6 jit_solution(6409033894757070523)
XLA Ops:
  7.9 2.4 stack.2
  10.3 9.4 %all-to-all-start = ((bf16[16,1,128,512]{3,2,1,0:T(8,128)(2,1)}), bf16[16,1,128,512]{3,2,1,0:T(8,128)(2,1)}, u32[]{:S(2)}, u32[]{:S(2)}) async-start(bf16[16,1,128,512]{3,2,1,0:T(8,128)(2,1)} %stack.2), calls=%async_computation | async-start | bytes 4194304 | tf_op jit(solution)/shard_map/all_to_all | solution.py:18
  24.1 88.5 %all-gather.2.cloned.1.call-done = bf16[1,2048,512]{2,1,0:T(8,128)(2,1)} async-done(((bf16[1,128,512]{2,1,0:T(8,128)(2,1)}), bf16[1,2048,512]{2,1,0:T(8,128)(2,1)}) %all-gather.2.cloned.1.call-update) | async-done | bytes 2097168 | tf_op jit(solution)/shard_map/all_gather | solution.py:82
  112.6 2.2 gather_fusion
  114.8 1.7 fusion.50
  116.6 1.8 fusion.51
  118.8 3.0 gather_fusion.1
  121.8 1.3 fusion.44
  126.4 1.7 fusion.9
  129.8 1.8 fusion.6
  133.2 1.4 fusion.3
  134.6 2.4 fusion.11
  141.9 4.0 %fusion.54 = f32[16,128,1024]{2,0,1:T(8,128)S(1)} fusion(f32[4,128,1024]{2,0,1:T(4,128)S(1)} %bitcast_dynamic-update-slice_fusion, s32[4]{0:T(128)S(1)} %bitcast.346), kind=kOutput, calls=%fused_computation.100 | convolution fusion | flops 100663360 | bytes 10485776 | tf_op jit(solution)/shard_map/cn,nrw->crw/dot_general | solution.py:122
  145.9 8.3 %copy.44 = f32[16,128,1024]{2,1,0:T(8,128)} copy(f32[16,128,1024]{2,0,1:T(8,128)S(1)} %fusion.54) | data formatting | bytes 16777216 | tf_op jit(solution)/shard_map/cn,nrw->crw/dot_general | solution.py:122
  154.3 1.2 copy-done.3
  155.5 1.3 fusion.31
  157.7 1.2 fusion.28
  159.1 1.3 fusion.29
  160.5 1.2 fusion.30
  162.0 6.8 %collective-permute-start = (bf16[1,128,4096]{2,1,0:T(8,128)(2,1)S(1)}, bf16[1,128,4096]{2,1,0:T(8,128)(2,1)S(1)}, u32[]{:S(2)}, u32[]{:S(2)}) collective-permute-start(bf16[1,128,4096]{2,1,0:T(8,128)(2,1)S(1)} %pad_maximum_fusion), channel_id=1, source_target_pairs={{0,240},{16,0},{32,16},{48,32},{64,48},{80,64},{96,80},{112,96},{1... | collective-permute-start | bytes 3145736 | tf_op jit(solution)/shard_map/ppermute | solution.py:24
  168.8 196.7 %reduce-scatter.2.cloned.1.call-done = f32[128,1024]{1,0:T(8,128)} async-done(((f32[2048,1024]{1,0:T(8,128)}), f32[128,1024]{1,0:T(8,128)}) %reduce-scatter.2.cloned.1.call-update) | async-done | bytes 524304 | tf_op jit(solution)/shard_map/reduce_scatter | solution.py:123
  365.5 1.1 convert_element_type.44
  367.2 3.9 %collective-permute-done.2 = bf16[1,128,512]{2,1,0:T(8,128)(2,1)S(1)} collective-permute-done((bf16[1,128,512]{2,1,0:T(8,128)(2,1)S(1)}, bf16[1,128,512]{2,1,0:T(8,128)(2,1)S(1)}, u32[]{:S(2)}, u32[]{:S(2)}) %collective-permute-start.2) | collective-permute-done | bytes 131104 | tf_op jit(solution)/shard_map/ppermute | solution.py:24
  371.1 1.4 collective-permute-done.1
  (97 shorter events, 20.1 us)
Async XLA Ops:
  7.2 105.5 %all-gather.2.cloned.1.call-start = ((), (), s32[]{:S(2)}) async-start(), calls=%async_computation.2 | async-start | bytes 2228224 | tf_op jit(solution)/shard_map/all_gather | solution.py:82
  10.3 10.2 %copy-start.15 = (bf16[1,128,4096]{2,1,0:T(8,128)(2,1)S(1)}, bf16[1,128,4096]{2,1,0:T(8,128)(2,1)}, u32[]{:S(2)}) copy-start(bf16[1,128,4096]{2,1,0:T(8,128)(2,1)} %param.7) | copy-start | bytes 3145732
  10.3 108.4 %all-to-all-start = ((bf16[16,1,128,512]{3,2,1,0:T(8,128)(2,1)}), bf16[16,1,128,512]{3,2,1,0:T(8,128)(2,1)}, u32[]{:S(2)}, u32[]{:S(2)}) async-start(bf16[16,1,128,512]{3,2,1,0:T(8,128)(2,1)} %stack.2), calls=%async_computation | async-start | bytes 4194304 | tf_op jit(solution)/shard_map/all_to_all | solution.py:18
  19.7 1.5 copy-start.16
  19.7 345.8 %reduce-scatter.2.cloned.1.call-start = ((), (), s32[]{:S(2)}) async-start(), calls=%async_computation.3 | async-start | bytes 8912896 | tf_op jit(solution)/shard_map/reduce_scatter | solution.py:123
  23.0 93.5 %copy-start.11 = (bf16[128,1024]{0,1:T(8,128)(2,1)}, bf16[128,1024]{0,1:T(8,128)(2,1)S(1)}, u32[]{:S(2)}) copy-start(bf16[128,1024]{0,1:T(8,128)(2,1)S(1)} %get-tuple-element.12) | copy-start | bytes 786436
  114.8 8.3 %copy-start.8 = (bf16[4,128,512]{2,1,0:T(8,128)(2,1)}, bf16[4,128,512]{2,1,0:T(8,128)(2,1)S(1)}, u32[]{:S(2)}) copy-start(bf16[4,128,512]{2,1,0:T(8,128)(2,1)S(1)} %gather_fusion) | copy-start | bytes 1572868
  114.8 3.5 copy-start.9
  118.3 3.5 copy-start.17
  118.8 4.4 %copy-start.13 = (bf16[128,1024]{0,1:T(8,128)(2,1)S(1)}, bf16[128,1024]{0,1:T(8,128)(2,1)}, u32[]{:S(2)}) copy-start(bf16[128,1024]{0,1:T(8,128)(2,1)} %get-tuple-element.15) | copy-start | bytes 786436
  124.1 1.6 copy-start.6
  124.1 2.2 copy-start.7
  124.1 2.3 copy-start.19
  134.6 2.5 copy-start.14
  134.6 2.9 copy-start.12
  137.1 1.6 copy-start
  137.1 1.6 copy-start.2
  139.4 1.7 copy-start.4
  155.5 2.2 copy-start.1
  156.8 2.3 copy-start.5
  159.1 2.8 copy-start.18
  162.0 205.1 %collective-permute-start = (bf16[1,128,4096]{2,1,0:T(8,128)(2,1)S(1)}, bf16[1,128,4096]{2,1,0:T(8,128)(2,1)S(1)}, u32[]{:S(2)}, u32[]{:S(2)}) collective-permute-start(bf16[1,128,4096]{2,1,0:T(8,128)(2,1)S(1)} %pad_maximum_fusion), channel_id=1, source_target_pairs={{0,240},{16,0},{32,16},{48,32},{64,48},{80,64},{96,80},{112,96},{1... | collective-permute-start | bytes 3145736 | tf_op jit(solution)/shard_map/ppermute | solution.py:24
  366.6 4.5 %collective-permute-start.2 = (bf16[1,128,512]{2,1,0:T(8,128)(2,1)S(1)}, bf16[1,128,512]{2,1,0:T(8,128)(2,1)S(1)}, u32[]{:S(2)}, u32[]{:S(2)}) collective-permute-start(bf16[1,128,512]{2,1,0:T(8,128)(2,1)S(1)} %get-tuple-element.20), channel_id=1, source_target_pairs={{0,240},{16,0},{32,16},{48,32},{64,48},{80,64},{96,80},{112,96},{1... | collective-permute-start | bytes 393224 | tf_op jit(solution)/shard_map/ppermute | solution.py:24
  367.1 5.4 %collective-permute-start.1 = (bf16[1,128,512]{2,1,0:T(8,128)(2,1)S(1)}, bf16[1,128,512]{2,1,0:T(8,128)(2,1)S(1)}, u32[]{:S(2)}, u32[]{:S(2)}) collective-permute-start(bf16[1,128,512]{2,1,0:T(8,128)(2,1)S(1)} %get-tuple-element.21), channel_id=1, source_target_pairs={{0,240},{16,0},{32,16},{48,32},{64,48},{80,64},{96,80},{112,96},{1... | collective-permute-start | bytes 393224 | tf_op jit(solution)/shard_map/ppermute | solution.py:24
  (7 other events, 8.1 us)
Sparse Core Ops, SparseCore 0:
  9.8 102.7 all-gather.1
  154.4 211.0 reduce-scatter.1
